TPU v7x, 32 devices: a whole 2x2x4 slice. The times are simulated.
32 devices in a mesh: ctx: 8 (over y, x, core), dp: 4 (over z).
Axes of the slice: x: 2, y: 2, z: 4, core: 2. Of those that a mesh axis runs over, the one named last changes fastest.
Arguments:
- hidden_in: bfloat16 [4, 2048, 2048], P('dp', 'ctx'), may hold values from -6 to 6
- queries: bfloat16 [4, 2048, 2048], P('dp', 'ctx'), may hold values from -1000 to 1000
- norm_gain: bfloat16 [2048], replicated, may hold values from 0.099609375 to 1.8984375
- weight_store: bfloat16 [4, 2048, 512], P('dp', 'ctx'), may hold values from -0.125 to 0.125
- owners: int32 [2], replicated, may hold values from 0 to 3, as said below
- doc_lengths: int32 [4, 4], P('dp'), may hold values from 1 to 1024, 2048 in all within a row
Outputs:
- attended: bfloat16 [4, 2048, 2048], P('dp', 'ctx')
Inputs may be any that keep to these rules, and one draw needn't show every extreme that they name: `owners`: two different data ranks, one of them the last rank 4 - 1; the first owns the key projection, the second the value projection.
All inputs are finite; a program needn't handle non-finite values.
Results may differ from a plain program's by a relative error of at most 0.012.
Values may be sent and summed in bfloat16 or wider, within the bound.
No kernel may reach another device: no remote copies, remote signals or barrier semaphores. Data moves between devices by JAX's collectives and lax.ppermute only.
A program may use at most 64 MiB of HBM per device.

v0:
```python
import jax
import jax.numpy as jnp
from jax import lax
from jax.sharding import PartitionSpec as P

HS = 128
REACH = 4


def from_root(block, axis, owner):
    block = jnp.where(lax.axis_index(axis) == owner, block, jnp.zeros_like(block))
    return lax.psum(block, axis)


def from_behind(x, axis, by):
    size = lax.axis_size(axis)
    pairs = [(i, i + by) for i in range(size) if 0 <= i + by < size]
    return lax.ppermute(x, axis, pairs)


def find_starts(lengths, positions):
    ends = jnp.cumsum(lengths)
    starts = ends - lengths
    below = starts[None, :] <= positions[:, None]
    return jnp.max(jnp.where(below, starts[None, :], 0), axis=1)


def copy_owner(slot_rows, owner):
    return from_root(slot_rows, "dp", owner)


def local(hidden_in, queries, norm_gain, weight_store, owners, doc_lengths):
    tok_rows = hidden_in.shape[1]
    key_width = weight_store.shape[2]
    kv_heads = key_width // HS
    group = queries.shape[2] // key_width
    width_all = (REACH + 1) * tok_rows
    ctx_index = lax.axis_index("ctx")
    xf = hidden_in[0].astype(jnp.float32)
    scaled = (
        xf
        * lax.rsqrt(jnp.mean(xf * xf, axis=-1, keepdims=True) + 1e-05)
        * norm_gain.astype(jnp.float32)
    ).astype(jnp.bfloat16)
    own_slot = weight_store[0]
    key_part = copy_owner(own_slot, owners[0])
    value_part = copy_owner(own_slot, owners[1])
    key_sum = jnp.dot(
        scaled,
        lax.all_gather(key_part, "ctx", axis=0, tiled=True),
        preferred_element_type=jnp.float32,
    )
    value_sum = jnp.dot(
        scaled,
        lax.all_gather(value_part, "ctx", axis=0, tiled=True),
        preferred_element_type=jnp.float32,
    )
    kv_own = jnp.stack([key_sum.astype(jnp.bfloat16), value_sum.astype(jnp.bfloat16)])
    earlier = [from_behind(kv_own, "ctx", back) for back in range(REACH, 0, -1)]
    window = jnp.concatenate(earlier + [kv_own], axis=1)
    q_pos = ctx_index * tok_rows + jnp.arange(tok_rows, dtype=jnp.int32)
    k_pos = (ctx_index - REACH) * tok_rows + jnp.arange(width_all, dtype=jnp.int32)
    q_start = find_starts(doc_lengths[0], q_pos)
    allowed = (k_pos[None, :] >= q_start[:, None]) & (k_pos[None, :] <= q_pos[:, None])
    q_heads = jnp.transpose(queries[0].reshape(tok_rows, kv_heads, group, HS), (1, 2, 0, 3))
    k_heads = jnp.transpose(window[0].reshape(width_all, kv_heads, HS), (1, 0, 2))
    v_heads = jnp.transpose(window[1].reshape(width_all, kv_heads, HS), (1, 0, 2))
    inverse_root = 1.0 / jnp.sqrt(jnp.float32(HS))

    def one_head(args):
        q_one, k_one, v_one = args
        rows = q_one.reshape(group * tok_rows, HS)
        score = jnp.dot(rows, k_one.T, preferred_element_type=jnp.float32)
        score = score.reshape(group, tok_rows, width_all) * inverse_root
        score = jnp.where(allowed[None], score, jnp.float32(-1e30))
        top = jnp.max(score, axis=-1, keepdims=True)
        weight = jnp.exp(score - top)
        total = jnp.sum(weight, axis=-1)
        weight_b = weight.astype(jnp.bfloat16).reshape(group * tok_rows, width_all)
        summed = jnp.dot(weight_b, v_one, preferred_element_type=jnp.float32)
        summed = summed.reshape(group, tok_rows, HS)
        return (summed / total[..., None]).astype(jnp.bfloat16)

    outputs = lax.map(one_head, (q_heads, k_heads, v_heads))
    attended = jnp.transpose(outputs, (2, 0, 1, 3)).reshape(1, tok_rows, kv_heads * group * HS)
    return attended


def solution(mesh):
    return jax.shard_map(
        local,
        mesh=mesh,
        in_specs=(
            P("dp", "ctx", None),
            P("dp", "ctx", None),
            P(),
            P("dp", "ctx", None),
            P(),
            P("dp", None),
        ),
        out_specs=P("dp", "ctx", None),
        check_vma=False,
    )
```

profile of v0, /device:TPU:1, one launch (start us, length us, event | category | flops | bytes accessed | tf_op | source)
XLA Modules:
  0.0 198.7 jit_solution(8778680894563662250)
XLA Ops:
  6.5 1.4 fusion.36
  9.3 1.8 select_bitcast_fusion.1
  11.1 39.7 %all-reduce.3.cloned.1.call-done = (bf16[256,512]{1,0:T(8,128)(2,1)}, bf16[256,512]{1,0:T(8,128)(2,1)}) async-done(((bf16[256,512]{1,0:T(8,128)(2,1)}, bf16[256,512]{1,0:T(8,128)(2,1)}), (bf16[256,512]{1,0:T(8,128)(2,1)}, bf16[256,512]{1,0:T(8,128)(2,1)})) %all-reduce.3.cloned.1.call-update) | async-done | bytes 524304 | tf_op jit(solution)/shard_map/psum | solution.py:12
  53.4 28.6 %all-gather.3.cloned.1.call-done = bf16[2048,512]{1,0:T(8,128)(2,1)} async-done(((bf16[256,512]{1,0:T(8,128)(2,1)}), bf16[2048,512]{1,0:T(8,128)(2,1)}) %all-gather.3.cloned.1.call-update) | async-done | bytes 2097168 | tf_op jit(solution)/shard_map/all_gather | solution.py:50
  82.0 2.3 %fusion.30 = bf16[1,256,512]{2,1,0:T(8,128)(2,1)S(1)} fusion(bf16[2048,512]{1,0:T(8,128)(2,1)} %all-gather.3.cloned.1.call-done, bf16[1,256,2048]{2,1,0:T(8,128)(2,1)S(1)} %copy-done, f32[2048]{0:T(1024)S(1)} %convert_element_type.26, f32[256]{0:T(256)S(1)} %add_rsqrt_fusion), kind=kOutput, calls=%fused_computation.29 | convolution fusion | flops 539099136 | bytes 3417088 | tf_op jit(solution)/shard_map/dot_general | solution.py:48
  84.4 27.5 %all-gather.5.cloned.1.call-done = bf16[2048,512]{1,0:T(8,128)(2,1)} async-done(((bf16[256,512]{1,0:T(8,128)(2,1)}), bf16[2048,512]{1,0:T(8,128)(2,1)}) %all-gather.5.cloned.1.call-update) | async-done | bytes 2097168 | tf_op jit(solution)/shard_map/all_gather | solution.py:55
  111.8 2.3 %fusion.31 = bf16[1,256,512]{2,1,0:T(8,128)(2,1)S(1)} fusion(bf16[2048,512]{1,0:T(8,128)(2,1)} %all-gather.5.cloned.1.call-done, bf16[1,256,2048]{2,1,0:T(8,128)(2,1)S(1)} %copy-done, f32[2048]{0:T(1024)S(1)} %convert_element_type.26, f32[256]{0:T(256)S(1)} %add_rsqrt_fusion), kind=kOutput, calls=%fused_computation.30 | convolution fusion | flops 539099136 | bytes 3417088 | tf_op jit(solution)/shard_map/dot_general | solution.py:53
  115.7 3.8 %collective-permute-start = (bf16[2,256,512]{2,1,0:T(8,128)(2,1)}, bf16[2,256,512]{2,1,0:T(8,128)(2,1)}, u32[]{:S(2)}, u32[]{:S(2)}) collective-permute-start(bf16[2,256,512]{2,1,0:T(8,128)(2,1)} %pad_maximum_fusion), channel_id=1, source_target_pairs={{0,16},{4,20},{8,24},{12,28},{1,17},{5,21},{9,25},{13,29},{2,18},{... | collective-permute-start | bytes 1572872 | tf_op jit(solution)/shard_map/ppermute | solution.py:18
  119.5 2.1 %collective-permute-start.1 = (bf16[2,256,512]{2,1,0:T(8,128)(2,1)}, bf16[2,256,512]{2,1,0:T(8,128)(2,1)}, u32[]{:S(2)}, u32[]{:S(2)}) collective-permute-start(bf16[2,256,512]{2,1,0:T(8,128)(2,1)} %pad_maximum_fusion), channel_id=1, source_target_pairs={{0,12},{4,16},{8,20},{12,24},{16,28},{1,13},{5,17},{9,21},{13,25},... | collective-permute-start | bytes 1572872 | tf_op jit(solution)/shard_map/ppermute | solution.py:18
  121.6 2.9 %collective-permute-start.2 = (bf16[2,256,512]{2,1,0:T(8,128)(2,1)}, bf16[2,256,512]{2,1,0:T(8,128)(2,1)}, u32[]{:S(2)}, u32[]{:S(2)}) collective-permute-start(bf16[2,256,512]{2,1,0:T(8,128)(2,1)} %pad_maximum_fusion), channel_id=1, source_target_pairs={{0,8},{4,12},{8,16},{12,20},{16,24},{20,28},{1,9},{5,13},{9,17},{1... | collective-permute-start | bytes 1572872 | tf_op jit(solution)/shard_map/ppermute | solution.py:18
  124.5 1.9 collective-permute-start.3
  127.1 25.4 %collective-permute-done = bf16[2,256,512]{2,1,0:T(8,128)(2,1)} collective-permute-done((bf16[2,256,512]{2,1,0:T(8,128)(2,1)}, bf16[2,256,512]{2,1,0:T(8,128)(2,1)}, u32[]{:S(2)}, u32[]{:S(2)}) %collective-permute-start) | collective-permute-done | bytes 524320 | tf_op jit(solution)/shard_map/ppermute | solution.py:18
  153.6 5.2 %collective-permute-done.1 = bf16[2,256,512]{2,1,0:T(8,128)(2,1)} collective-permute-done((bf16[2,256,512]{2,1,0:T(8,128)(2,1)}, bf16[2,256,512]{2,1,0:T(8,128)(2,1)}, u32[]{:S(2)}, u32[]{:S(2)}) %collective-permute-start.1) | collective-permute-done | bytes 524320 | tf_op jit(solution)/shard_map/ppermute | solution.py:18
  163.4 3.6 %reshape_squeeze.10 = bf16[1280,4,128]{2,1,0:T(4,128)(2,1)} reshape(bf16[1,1280,512]{2,1,0:T(8,128)(2,1)} %get-tuple-element.96) | data formatting | bytes 2621440 | tf_op jit(solution)/shard_map/reshape;squeeze | solution.py:66
  168.2 3.1 %copy_bitcast_fusion = (bf16[4,1280,128]{2,1,0:T(8,128)(2,1)}, bf16[4,1280,128]{2,1,0:T(8,128)(2,1)S(1)}) fusion(bf16[1280,4,128]{2,1,0:T(4,128)(2,1)} %reshape_squeeze.11, bf16[1280,4,128]{2,1,0:T(4,128)(2,1)} %reshape_squeeze.10), kind=kLoop, calls=%fused_computation.25 | loop fusion | bytes 5242880 | tf_op jit(solution)/shard_map/transpose | solution.py:67
  171.3 18.5 %while.11 = (s32[]{:T(128)}, bf16[4,4,256,128]{3,2,1,0:T(8,128)(2,1)S(1)}, bf16[4,4,256,128]{2,3,1,0:T(8,128)(2,1)S(1)}, bf16[4,1280,128]{2,1,0:T(8,128)(2,1)S(1...) while((s32[]{:T(128)}, ...), condition=%wide.region_8.9_spmd.clone, body=%wide.region_5.8_spmd.clone.sunk | while | flops 681506816 | bytes 17593436 | solution.py:84
  173.9 2.0 %fusion.48 = bf16[4,4,256,128]{3,2,1,0:T(8,128)(2,1)S(1)} fusion(bf16[4,4,256,128]{3,2,1,0:T(8,128)(2,1)S(1)} %get-tuple-element.166, s32[]{:T(128)} %get-tuple-element.165, f32[4,256,1280]{2,1,0:T(8,128)S(1)} %get-tuple-element.154, f32[4,256]{1,0:T(4,128)S(1)} %get-tuple-element.155, bf16[4,1280,128]{2,1,0:T(8,128)(2,1)} %get-tuple-element.178, ...), kind=kOutput, calls=%fused_computation.11.clone.1 | convolution fusion | flops 338427904 | bytes 5841920 | tf_op jit(solution)/shard_map/while/body/eval_jaxpr/dot_general | solution.py:80
  176.2 1.3 fusion.46
  178.5 2.0 %fusion.48 = bf16[4,4,256,128]{3,2,1,0:T(8,128)(2,1)S(1)} fusion(bf16[4,4,256,128]{3,2,1,0:T(8,128)(2,1)S(1)} %get-tuple-element.166, s32[]{:T(128)} %get-tuple-element.165, f32[4,256,1280]{2,1,0:T(8,128)S(1)} %get-tuple-element.154, f32[4,256]{1,0:T(4,128)S(1)} %get-tuple-element.155, bf16[4,1280,128]{2,1,0:T(8,128)(2,1)} %get-tuple-element.178, ...), kind=kOutput, calls=%fused_computation.11.clone.1 | convolution fusion | flops 338427904 | bytes 5841920 | tf_op jit(solution)/shard_map/while/body/eval_jaxpr/dot_general | solution.py:80
  180.8 1.3 fusion.46
  183.1 2.0 %fusion.48 = bf16[4,4,256,128]{3,2,1,0:T(8,128)(2,1)S(1)} fusion(bf16[4,4,256,128]{3,2,1,0:T(8,128)(2,1)S(1)} %get-tuple-element.166, s32[]{:T(128)} %get-tuple-element.165, f32[4,256,1280]{2,1,0:T(8,128)S(1)} %get-tuple-element.154, f32[4,256]{1,0:T(4,128)S(1)} %get-tuple-element.155, bf16[4,1280,128]{2,1,0:T(8,128)(2,1)} %get-tuple-element.178, ...), kind=kOutput, calls=%fused_computation.11.clone.1 | convolution fusion | flops 338427904 | bytes 5841920 | tf_op jit(solution)/shard_map/while/body/eval_jaxpr/dot_general | solution.py:80
  185.5 1.3 fusion.46
  187.7 2.0 %fusion.48 = bf16[4,4,256,128]{3,2,1,0:T(8,128)(2,1)S(1)} fusion(bf16[4,4,256,128]{3,2,1,0:T(8,128)(2,1)S(1)} %get-tuple-element.166, s32[]{:T(128)} %get-tuple-element.165, f32[4,256,1280]{2,1,0:T(8,128)S(1)} %get-tuple-element.154, f32[4,256]{1,0:T(4,128)S(1)} %get-tuple-element.155, bf16[4,1280,128]{2,1,0:T(8,128)(2,1)} %get-tuple-element.178, ...), kind=kOutput, calls=%fused_computation.11.clone.1 | convolution fusion | flops 338427904 | bytes 5841920 | tf_op jit(solution)/shard_map/while/body/eval_jaxpr/dot_general | solution.py:80
  190.6 1.6 reshape.47
  (46 shorter events, 18.9 us)
Async XLA Ops:
  6.5 46.5 %copy-start = (bf16[1,256,2048]{2,1,0:T(8,128)(2,1)S(1)}, bf16[1,256,2048]{2,1,0:T(8,128)(2,1)}, u32[]{:S(2)}) copy-start(bf16[1,256,2048]{2,1,0:T(8,128)(2,1)} %param.8) | copy-start | bytes 3145732
  6.5 44.3 %all-reduce.3.cloned.1.call-start = ((), (), s32[]{:S(2)}) async-start(), calls=%async_computation.2 | async-start | bytes 1048576 | tf_op jit(solution)/shard_map/psum | solution.py:12
  11.1 70.9 %all-gather.3.cloned.1.call-start = ((), (), s32[]{:S(2)}) async-start(), calls=%async_computation | async-start | bytes 2359296 | tf_op jit(solution)/shard_map/all_gather | solution.py:50
  50.8 61.0 %all-gather.5.cloned.1.call-start = ((), (), s32[]{:S(2)}) async-start(), calls=%async_computation.1 | async-start | bytes 2359296 | tf_op jit(solution)/shard_map/all_gather | solution.py:55
  84.3 37.3 %copy-start.4 = (s32[1,4]{1,0:T(1,128)S(1)}, s32[1,4]{1,0:T(1,128)}, u32[]{:S(2)}) copy-start(s32[1,4]{1,0:T(1,128)} %param.13) | copy-start | bytes 52
  84.3 42.1 %copy-start.1 = (bf16[1,256,2048]{2,1,0:T(8,128)(2,1)S(1)}, bf16[1,256,2048]{2,1,0:T(8,128)(2,1)}, u32[]{:S(2)}) copy-start(bf16[1,256,2048]{2,1,0:T(8,128)(2,1)} %param.9) | copy-start | bytes 3145732
  114.2 0.7 copy-start.2
  115.7 36.8 %collective-permute-start = (bf16[2,256,512]{2,1,0:T(8,128)(2,1)}, bf16[2,256,512]{2,1,0:T(8,128)(2,1)}, u32[]{:S(2)}, u32[]{:S(2)}) collective-permute-start(bf16[2,256,512]{2,1,0:T(8,128)(2,1)} %pad_maximum_fusion), channel_id=1, source_target_pairs={{0,16},{4,20},{8,24},{12,28},{1,17},{5,21},{9,25},{13,29},{2,18},{... | collective-permute-start | bytes 1572872 | tf_op jit(solution)/shard_map/ppermute | solution.py:18
  119.5 39.3 %collective-permute-start.1 = (bf16[2,256,512]{2,1,0:T(8,128)(2,1)}, bf16[2,256,512]{2,1,0:T(8,128)(2,1)}, u32[]{:S(2)}, u32[]{:S(2)}) collective-permute-start(bf16[2,256,512]{2,1,0:T(8,128)(2,1)} %pad_maximum_fusion), channel_id=1, source_target_pairs={{0,12},{4,16},{8,20},{12,24},{16,28},{1,13},{5,17},{9,21},{13,25},... | collective-permute-start | bytes 1572872 | tf_op jit(solution)/shard_map/ppermute | solution.py:18
  121.6 38.3 %collective-permute-start.2 = (bf16[2,256,512]{2,1,0:T(8,128)(2,1)}, bf16[2,256,512]{2,1,0:T(8,128)(2,1)}, u32[]{:S(2)}, u32[]{:S(2)}) collective-permute-start(bf16[2,256,512]{2,1,0:T(8,128)(2,1)} %pad_maximum_fusion), channel_id=1, source_target_pairs={{0,8},{4,12},{8,16},{12,20},{16,24},{20,28},{1,9},{5,13},{9,17},{1... | collective-permute-start | bytes 1572872 | tf_op jit(solution)/shard_map/ppermute | solution.py:18
  124.5 36.5 %collective-permute-start.3 = (bf16[2,256,512]{2,1,0:T(8,128)(2,1)}, bf16[2,256,512]{2,1,0:T(8,128)(2,1)}, u32[]{:S(2)}, u32[]{:S(2)}) collective-permute-start(bf16[2,256,512]{2,1,0:T(8,128)(2,1)} %pad_maximum_fusion), channel_id=1, source_target_pairs={{0,4},{4,8},{8,12},{12,16},{16,20},{20,24},{24,28},{1,5},{5,9},{9,... | collective-permute-start | bytes 1572872 | tf_op jit(solution)/shard_map/ppermute | solution.py:18
  127.1 35.0 %copy-start.3 = (bf16[1,256,512]{2,1,0:T(8,128)(2,1)S(1)}, bf16[1,256,512]{2,1,0:T(8,128)(2,1)}, u32[]{:S(2)}) copy-start(bf16[1,256,512]{2,1,0:T(8,128)(2,1)} %copy-done.2) | copy-start | bytes 786436
Sparse Core Ops, SparseCore 0:
  11.2 39.5 all-reduce.2
  52.7 29.2 all-gather.2
  83.9 27.8 all-gather.4
where the time goes:
time: 199 us
  waiting for transfers between devices  127 us (64%)
  local copies, waits for them, and re-layouts  18.5 us (9%)
  matrix products  17.9 us (9%)
  between operations  14.6 us (7%)
  starting transfers between devices  10.8 us (5%)
  other arithmetic  9.72 us (5%)
    psum x1, waiting for transfers between devices, from_root(): return lax.psum(block, axis)  39.7 us
    ppermute x4, waiting for transfers between devices, from_behind(): return lax.ppermute(x, axis, pairs)  30.6 us
    all_gather x1, waiting for transfers between devices, local(): lax.all_gather(key_part, 'ctx', axis=0, tiled=True)  28.6 us
    all_gather x1, waiting for transfers between devices, local(): lax.all_gather(value_part, 'ctx', axis=0, tiled=True)  27.5 us
    ppermute x4, starting transfers between devices, from_behind(): return lax.ppermute(x, axis, pairs)  10.7 us
    dot_general x4, matrix products, one_head(): summed = jnp.dot(weight_b, v_one, preferred_element_type=jnp.float32)  8.07 us
    unnamed x15, local copies, waits for them, and re-layouts  5.55 us
    dot_general x4, matrix products, one_head(): score = jnp.dot(rows, k_one.T, preferred_element_type=jnp.float32)  5.14 us
  transfers between devices with their start and end apart: 7, of which 5 were waited for; matrix products, arithmetic and copies ran while one was open for 4% of the time, Pallas kernels for 0%

commit v1 on v0

--- a/solution.py
+++ b/solution.py
@@ -7,9 +7,15 @@
 REACH = 4
 
 
+def gather_and_add(x, mesh_axis):
+    parts = lax.all_gather(x, mesh_axis, axis=0, tiled=False)
+    summed = parts.sum(axis=0)
+    return summed
+
+
 def from_root(block, axis, owner):
     block = jnp.where(lax.axis_index(axis) == owner, block, jnp.zeros_like(block))
-    return lax.psum(block, axis)
+    return gather_and_add(block, axis)
 
 
 def from_behind(x, axis, by):

time: 199 us -> 217 us (1.090)
  waiting for transfers between devices: 127 us -> 142 us
  other arithmetic: 9.72 us -> 12.8 us
    all_gather x0 -> x2, waiting for transfers between devices: none -> 56 us  [gather_and_add(): parts = lax.all_gather(x, mesh_axis, axis=0, tiled=False)]
    psum x1 -> x0, waiting for transfers between devices: 39.7 us -> none  [from_root(): return lax.psum(block, axis)]
    reduce_sum x0 -> x2, other arithmetic: none -> 4.31 us  [gather_and_add(): summed = parts.sum(axis=0)]
    unnamed x15 -> x17, local copies, waits for them, and re-layouts: 5.55 us -> 5.55 us
  transfers between devices with their start and end apart: 7 -> 8, of which waited for: 5 -> 6; matrix products, arithmetic and copies ran while one was open for 4% -> 5% of each run, Pallas kernels for 0% -> 0%
where the time goes in v1:
time: 217 us; the launch traced here: 216 us
  waiting for transfers between devices  142 us (65%)
  local copies, waits for them, and re-layouts  18.4 us (8%)
  matrix products  17.9 us (8%)
  between operations  14.5 us (7%)
  other arithmetic  12.8 us (6%)
  starting transfers between devices  10.9 us (5%)
    all_gather x2, waiting for transfers between devices, gather_and_add(): parts = lax.all_gather(x, mesh_axis, axis=0, tiled=False)  56 us
    ppermute x4, waiting for transfers between devices, from_behind(): return lax.ppermute(x, axis, pairs)  30.6 us
    all_gather x1, waiting for transfers between devices, local(): lax.all_gather(value_part, 'ctx', axis=0, tiled=True)  27.3 us
    all_gather x1, waiting for transfers between devices, local(): lax.all_gather(key_part, 'ctx', axis=0, tiled=True)  27.2 us
    ppermute x4, starting transfers between devices, from_behind(): return lax.ppermute(x, axis, pairs)  10.7 us
    dot_general x4, matrix products, one_head(): summed = jnp.dot(weight_b, v_one, preferred_element_type=jnp.float32)  8.07 us
    unnamed x17, local copies, waits for them, and re-layouts  5.55 us
    dot_general x4, matrix products, one_head(): score = jnp.dot(rows, k_one.T, preferred_element_type=jnp.float32)  5.14 us
  transfers between devices with their start and end apart: 8, of which 6 were waited for; matrix products, arithmetic and copies ran while one was open for 5% of the time, Pallas kernels for 0%

profile of v1, /device:TPU:1, one launch (start us, length us, event | category | flops | bytes accessed | tf_op | source)
XLA Modules:
  0.0 216.5 jit_solution(1968186750473574653)
XLA Ops:
  6.5 1.3 fusion.36
  9.1 1.9 broadcast_select_fusion.1
  11.8 29.2 %all-gather.5.cloned.1.call-done = bf16[4,256,512]{2,1,0:T(8,128)(2,1)} async-done(((bf16[1,256,512]{2,1,0:T(8,128)(2,1)}), bf16[4,256,512]{2,1,0:T(8,128)(2,1)}) %all-gather.5.cloned.1.call-update) | async-done | bytes 1048592 | tf_op jit(solution)/shard_map/all_gather | solution.py:11
  41.0 2.2 reduce_sum.43
  43.2 26.8 %all-gather.9.cloned.1.call-done = bf16[4,256,512]{2,1,0:T(8,128)(2,1)} async-done(((bf16[1,256,512]{2,1,0:T(8,128)(2,1)}), bf16[4,256,512]{2,1,0:T(8,128)(2,1)}) %all-gather.9.cloned.1.call-update) | async-done | bytes 1048592 | tf_op jit(solution)/shard_map/all_gather | solution.py:11
  70.0 2.2 reduce_sum.44
  72.7 27.2 %all-gather.7.cloned.1.call-done = bf16[2048,512]{1,0:T(8,128)(2,1)} async-done(((bf16[256,512]{1,0:T(8,128)(2,1)}), bf16[2048,512]{1,0:T(8,128)(2,1)}) %all-gather.7.cloned.1.call-update) | async-done | bytes 2097168 | tf_op jit(solution)/shard_map/all_gather | solution.py:56
  99.9 2.3 %fusion.30 = bf16[1,256,512]{2,1,0:T(8,128)(2,1)S(1)} fusion(bf16[2048,512]{1,0:T(8,128)(2,1)} %all-gather.7.cloned.1.call-done, bf16[1,256,2048]{2,1,0:T(8,128)(2,1)S(1)} %copy-done, f32[2048]{0:T(1024)S(1)} %convert_element_type.30, f32[256]{0:T(256)S(1)} %add_rsqrt_fusion), kind=kOutput, calls=%fused_computation.29 | convolution fusion | flops 539099136 | bytes 3417088 | tf_op jit(solution)/shard_map/dot_general | solution.py:54
  102.3 27.3 %all-gather.11.cloned.1.call-done = bf16[2048,512]{1,0:T(8,128)(2,1)} async-done(((bf16[256,512]{1,0:T(8,128)(2,1)}), bf16[2048,512]{1,0:T(8,128)(2,1)}) %all-gather.11.cloned.1.call-update) | async-done | bytes 2097168 | tf_op jit(solution)/shard_map/all_gather | solution.py:61
  129.6 2.3 %fusion.31 = bf16[1,256,512]{2,1,0:T(8,128)(2,1)S(1)} fusion(bf16[2048,512]{1,0:T(8,128)(2,1)} %all-gather.11.cloned.1.call-done, bf16[1,256,2048]{2,1,0:T(8,128)(2,1)S(1)} %copy-done, f32[2048]{0:T(1024)S(1)} %convert_element_type.30, f32[256]{0:T(256)S(1)} %add_rsqrt_fusion), kind=kOutput, calls=%fused_computation.30 | convolution fusion | flops 539099136 | bytes 3417088 | tf_op jit(solution)/shard_map/dot_general | solution.py:59
  133.5 3.8 %collective-permute-start = (bf16[2,256,512]{2,1,0:T(8,128)(2,1)}, bf16[2,256,512]{2,1,0:T(8,128)(2,1)}, u32[]{:S(2)}, u32[]{:S(2)}) collective-permute-start(bf16[2,256,512]{2,1,0:T(8,128)(2,1)} %pad_maximum_fusion), channel_id=1, source_target_pairs={{0,16},{4,20},{8,24},{12,28},{1,17},{5,21},{9,25},{13,29},{2,18},{... | collective-permute-start | bytes 1572872 | tf_op jit(solution)/shard_map/ppermute | solution.py:24
  137.3 2.1 collective-permute-start.1
  139.3 3.0 %collective-permute-start.2 = (bf16[2,256,512]{2,1,0:T(8,128)(2,1)}, bf16[2,256,512]{2,1,0:T(8,128)(2,1)}, u32[]{:S(2)}, u32[]{:S(2)}) collective-permute-start(bf16[2,256,512]{2,1,0:T(8,128)(2,1)} %pad_maximum_fusion), channel_id=1, source_target_pairs={{0,8},{4,12},{8,16},{12,20},{16,24},{20,28},{1,9},{5,13},{9,17},{1... | collective-permute-start | bytes 1572872 | tf_op jit(solution)/shard_map/ppermute | solution.py:24
  142.3 1.9 collective-permute-start.3
  144.9 25.4 %collective-permute-done = bf16[2,256,512]{2,1,0:T(8,128)(2,1)} collective-permute-done((bf16[2,256,512]{2,1,0:T(8,128)(2,1)}, bf16[2,256,512]{2,1,0:T(8,128)(2,1)}, u32[]{:S(2)}, u32[]{:S(2)}) %collective-permute-start) | collective-permute-done | bytes 524320 | tf_op jit(solution)/shard_map/ppermute | solution.py:24
  171.3 5.3 %collective-permute-done.1 = bf16[2,256,512]{2,1,0:T(8,128)(2,1)} collective-permute-done((bf16[2,256,512]{2,1,0:T(8,128)(2,1)}, bf16[2,256,512]{2,1,0:T(8,128)(2,1)}, u32[]{:S(2)}, u32[]{:S(2)}) %collective-permute-start.1) | collective-permute-done | bytes 524320 | tf_op jit(solution)/shard_map/ppermute | solution.py:24
  181.2 3.6 %reshape_squeeze.10 = bf16[1280,4,128]{2,1,0:T(4,128)(2,1)} reshape(bf16[1,1280,512]{2,1,0:T(8,128)(2,1)} %get-tuple-element.102) | data formatting | bytes 2621440 | tf_op jit(solution)/shard_map/reshape;squeeze | solution.py:72
  185.9 3.1 %copy_bitcast_fusion = (bf16[4,1280,128]{2,1,0:T(8,128)(2,1)}, bf16[4,1280,128]{2,1,0:T(8,128)(2,1)S(1)}) fusion(bf16[1280,4,128]{2,1,0:T(4,128)(2,1)} %reshape_squeeze.11, bf16[1280,4,128]{2,1,0:T(4,128)(2,1)} %reshape_squeeze.10), kind=kLoop, calls=%fused_computation.25 | loop fusion | bytes 5242880 | tf_op jit(solution)/shard_map/transpose | solution.py:73
  189.1 18.5 %while.11 = (s32[]{:T(128)}, bf16[4,4,256,128]{3,2,1,0:T(8,128)(2,1)S(1)}, bf16[4,4,256,128]{2,3,1,0:T(8,128)(2,1)S(1)}, bf16[4,1280,128]{2,1,0:T(8,128)(2,1)S(1...) while((s32[]{:T(128)}, ...), condition=%wide.region_8.9_spmd.clone, body=%wide.region_5.8_spmd.clone.sunk | while | flops 681506816 | bytes 17593436 | solution.py:90
  191.6 2.0 fusion.48
  196.3 2.0 fusion.48
  200.9 2.0 fusion.48
  205.5 2.0 fusion.48
  208.3 1.6 reshape.41
  (53 shorter events, 21.4 us)
Async XLA Ops:
  6.5 34.5 %all-gather.5.cloned.1.call-start = ((), (), s32[]{:S(2)}) async-start(), calls=%async_computation | async-start | bytes 1310720 | tf_op jit(solution)/shard_map/all_gather | solution.py:11
  9.1 63.2 %copy-start.4 = (bf16[2048]{0:T(1024)(128)(2,1)S(1)}, bf16[2048]{0:T(1024)(128)(2,1)}, u32[]{:S(2)}) copy-start(bf16[2048]{0:T(1024)(128)(2,1)} %param.10) | copy-start | bytes 12292
  9.1 63.2 %copy-start.5 = (s32[1,4]{1,0:T(1,128)S(1)}, s32[1,4]{1,0:T(1,128)}, u32[]{:S(2)}) copy-start(s32[1,4]{1,0:T(1,128)} %param.13) | copy-start | bytes 52
  9.1 63.3 %copy-start = (bf16[1,256,2048]{2,1,0:T(8,128)(2,1)S(1)}, bf16[1,256,2048]{2,1,0:T(8,128)(2,1)}, u32[]{:S(2)}) copy-start(bf16[1,256,2048]{2,1,0:T(8,128)(2,1)} %param.8) | copy-start | bytes 3145732
  11.0 59.1 %all-gather.9.cloned.1.call-start = ((), (), s32[]{:S(2)}) async-start(), calls=%async_computation.2 | async-start | bytes 1310720 | tf_op jit(solution)/shard_map/all_gather | solution.py:11
  11.7 88.2 %all-gather.7.cloned.1.call-start = ((), (), s32[]{:S(2)}) async-start(), calls=%async_computation.1 | async-start | bytes 2359296 | tf_op jit(solution)/shard_map/all_gather | solution.py:56
  43.2 86.4 %all-gather.11.cloned.1.call-start = ((), (), s32[]{:S(2)}) async-start(), calls=%async_computation.3 | async-start | bytes 2359296 | tf_op jit(solution)/shard_map/all_gather | solution.py:61
  102.3 42.0 %copy-start.1 = (bf16[1,256,2048]{2,1,0:T(8,128)(2,1)S(1)}, bf16[1,256,2048]{2,1,0:T(8,128)(2,1)}, u32[]{:S(2)}) copy-start(bf16[1,256,2048]{2,1,0:T(8,128)(2,1)} %param.9) | copy-start | bytes 3145732
  131.9 0.7 copy-start.2
  133.5 36.8 %collective-permute-start = (bf16[2,256,512]{2,1,0:T(8,128)(2,1)}, bf16[2,256,512]{2,1,0:T(8,128)(2,1)}, u32[]{:S(2)}, u32[]{:S(2)}) collective-permute-start(bf16[2,256,512]{2,1,0:T(8,128)(2,1)} %pad_maximum_fusion), channel_id=1, source_target_pairs={{0,16},{4,20},{8,24},{12,28},{1,17},{5,21},{9,25},{13,29},{2,18},{... | collective-permute-start | bytes 1572872 | tf_op jit(solution)/shard_map/ppermute | solution.py:24
  137.3 39.3 %collective-permute-start.1 = (bf16[2,256,512]{2,1,0:T(8,128)(2,1)}, bf16[2,256,512]{2,1,0:T(8,128)(2,1)}, u32[]{:S(2)}, u32[]{:S(2)}) collective-permute-start(bf16[2,256,512]{2,1,0:T(8,128)(2,1)} %pad_maximum_fusion), channel_id=1, source_target_pairs={{0,12},{4,16},{8,20},{12,24},{16,28},{1,13},{5,17},{9,21},{13,25},... | collective-permute-start | bytes 1572872 | tf_op jit(solution)/shard_map/ppermute | solution.py:24
  139.3 38.3 %collective-permute-start.2 = (bf16[2,256,512]{2,1,0:T(8,128)(2,1)}, bf16[2,256,512]{2,1,0:T(8,128)(2,1)}, u32[]{:S(2)}, u32[]{:S(2)}) collective-permute-start(bf16[2,256,512]{2,1,0:T(8,128)(2,1)} %pad_maximum_fusion), channel_id=1, source_target_pairs={{0,8},{4,12},{8,16},{12,20},{16,24},{20,28},{1,9},{5,13},{9,17},{1... | collective-permute-start | bytes 1572872 | tf_op jit(solution)/shard_map/ppermute | solution.py:24
  142.3 36.5 %collective-permute-start.3 = (bf16[2,256,512]{2,1,0:T(8,128)(2,1)}, bf16[2,256,512]{2,1,0:T(8,128)(2,1)}, u32[]{:S(2)}, u32[]{:S(2)}) collective-permute-start(bf16[2,256,512]{2,1,0:T(8,128)(2,1)} %pad_maximum_fusion), channel_id=1, source_target_pairs={{0,4},{4,8},{8,12},{12,16},{16,20},{20,24},{24,28},{1,5},{5,9},{9,... | collective-permute-start | bytes 1572872 | tf_op jit(solution)/shard_map/ppermute | solution.py:24
  144.9 35.0 %copy-start.3 = (bf16[1,256,512]{2,1,0:T(8,128)(2,1)S(1)}, bf16[1,256,512]{2,1,0:T(8,128)(2,1)}, u32[]{:S(2)}) copy-start(bf16[1,256,512]{2,1,0:T(8,128)(2,1)} %copy-done.2) | copy-start | bytes 786436
Sparse Core Ops, SparseCore 0:
  11.1 29.8 all-gather.4
  42.6 27.4 all-gather.8
  71.9 27.9 all-gather.6
  101.7 27.8 all-gather.10
